TPU v7x, 256 devices: a whole 4x4x8 slice. The times are simulated.
256 devices in a mesh: gz: 2 (over core), row: 4 (over x), col: 32 (over z, y).
Axes of the slice: x: 4, y: 4, z: 8, core: 2. Of those that a mesh axis runs over, the one named last changes fastest.
Arguments:
- ancestor: float32 [4096, 16384], P('row', 'col'), may hold values from -6 to 6
- lower_panel: bfloat16 [2, 64, 24, 128, 128], P('gz', 'col', 'row'), may hold values from -6 to 6
- row_ids: int32 [2, 64, 24], P('gz', 'col', 'row'), may hold values from 0 to 7, as said below
- row_counts: int32 [2, 64, 4], P('gz', 'col', 'row'), may hold values from 1 to 6
- diag_inverse: bfloat16 [2, 64, 128, 128], P('gz', 'col'), may hold values from -0.5 to 0.5
- upper_panel: bfloat16 [2, 64, 96, 128, 128], P('gz', 'row', 'col'), may hold values from -0.1875 to 0.1875
- col_ids: int32 [2, 64, 96], P('gz', 'row', 'col'), may hold values from 0 to 3, as said below
- col_counts: int32 [2, 64, 32], P('gz', 'row', 'col'), may hold values from 1 to 3
Outputs:
- updated: float32 [4096, 16384], P('row', 'col')
Inputs may be any that keep to these rules, and one draw needn't show every extreme that they name: `row_ids`: within each layer, supernode and process row the 6 slots name distinct local block rows. `col_ids`: within each layer, supernode and process column the 3 slots name distinct local block columns.
All inputs are finite; a program needn't handle non-finite values.
Results may differ from a plain program's by a relative error of at most 0.0026.
Values may be sent and summed in bfloat16 or wider, within the bound.
A program may use at most 128 MiB of HBM per device.

v0:
```python
import jax
import jax.numpy as jnp
from jax import lax
from jax.sharding import PartitionSpec as P


def spread_rows(tiles, ids, counts, blocks):
    slots = ids.shape[1]
    slot_index = jnp.arange(slots, dtype=jnp.int32)
    alive = slot_index[None, :] < counts
    target = jnp.arange(blocks, dtype=jnp.int32)
    select = ((ids[:, :, None] == target[None, None, :]) & alive[:, :, None]).astype(jnp.bfloat16)
    dense = jnp.einsum("krl,krab->lakb", select, tiles, preferred_element_type=jnp.float32).astype(
        jnp.bfloat16
    )
    width = tiles.shape[-1]
    return dense.reshape(blocks * width, tiles.shape[0] * width)


def spread_cols(tiles, ids, counts, blocks):
    slots = ids.shape[1]
    slot_index = jnp.arange(slots, dtype=jnp.int32)
    alive = slot_index[None, :] < counts
    target = jnp.arange(blocks, dtype=jnp.int32)
    select = ((ids[:, :, None] == target[None, None, :]) & alive[:, :, None]).astype(jnp.bfloat16)
    dense = jnp.einsum("kcm,kcab->kamb", select, tiles, preferred_element_type=jnp.float32).astype(
        jnp.bfloat16
    )
    width = tiles.shape[-1]
    return dense.reshape(tiles.shape[0] * width, blocks * width)


def on_device(
    ancestor, lower_panel, row_ids, row_counts, diag_inverse, upper_panel, col_ids, col_counts
):
    width = lower_panel.shape[-1]
    row_blocks = ancestor.shape[0] // width
    col_blocks = ancestor.shape[1] // width
    solved = jnp.einsum(
        "ksab,kbc->ksac", lower_panel[0], diag_inverse[0], preferred_element_type=jnp.float32
    ).astype(jnp.bfloat16)
    piece = lax.all_gather((upper_panel[0], col_ids[0], col_counts[0]), "row", axis=0, tiled=True)
    upper_dense = spread_cols(piece[0], piece[1], piece[2], col_blocks)
    piece = lax.all_gather((solved, row_ids[0], row_counts[0]), "col", axis=0, tiled=True)
    lower_dense = spread_rows(piece[0], piece[1], piece[2], row_blocks)
    partial_sum = jnp.dot(lower_dense, upper_dense, preferred_element_type=jnp.float32)
    return ancestor - lax.psum(partial_sum, "gz")


def solution(mesh):
    placed = (
        P("row", "col"),
        P("gz", "col", "row", None, None),
        P("gz", "col", "row"),
        P("gz", "col", "row"),
        P("gz", "col", None, None),
        P("gz", "row", "col", None, None),
        P("gz", "row", "col"),
        P("gz", "row", "col"),
    )
    return jax.shard_map(
        on_device, mesh=mesh, in_specs=placed, out_specs=P("row", "col"), check_vma=False
    )
```

profile of v0, /device:TPU:1, one launch (start us, length us, event | category | flops | bytes accessed | tf_op | source)
XLA Modules:
  0.0 301.7 jit_solution(158132594757815860)
XLA Ops:
  6.5 0.0 copy-start
  6.5 0.0 all-gather.10.cloned.1.call-start
  6.5 0.7 all-gather.10.cloned.1.call-update
  7.3 0.0 all-gather.8.cloned.1.call-start
  7.3 0.2 copy-done
  7.5 1.8 convolution_convert_fusion
  9.4 0.0 all-gather.8.cloned.1.call-update
  9.4 0.0 all-reduce.4.cloned.1.call-start
  9.4 1.3 dynamic-slice
  10.8 1.3 dynamic-slice.1
  12.1 0.8 copy.17
  14.2 0.8 bitcast_dynamic-update-slice_fusion.1
  14.9 20.0 %all-reduce = s32[64]{0:T(128)S(1)} all-reduce(s32[64]{0:T(128)S(1)} %bitcast_dynamic-update-slice_fusion.1), channel_id=3, replica_groups=mesh['gz'=2,'row'=4,'col'=32] {'col'}, use_global_device_ids=true, to_apply=%add | all-reduce | flops 64 | bytes 512
  35.0 0.7 bitcast_dynamic-update-slice_fusion
  35.7 7.7 %all-reduce.1 = s32[64]{0:T(128)S(1)} all-reduce(s32[64]{0:T(128)S(1)} %bitcast_dynamic-update-slice_fusion), channel_id=5, replica_groups=mesh['gz'=2,'row'=4,'col'=32] {'row'}, use_global_device_ids=true, to_apply=%add.1 | all-reduce | flops 64 | bytes 512
  43.4 10.6 %all-gather.2 = s32[1,64,3]{2,0,1:T(1,128)S(1)} all-gather(s32[1,16,3]{2,0,1:T(1,128)S(1)} %copy.17), channel_id=4, replica_groups=mesh['gz'=2,'row'=4,'col'=32] {'row'}, dimensions={1}, use_global_device_ids=true | all-gather | bytes 960 | tf_op jit(solution)/shard_map/all_gather | solution.py:42
  54.0 35.0 %all-gather = s32[1,64,6]{2,0,1:T(1,128)S(1)} all-gather(s32[1,2,6]{2,0,1:T(1,128)} %bitcast.51), channel_id=2, replica_groups=mesh['gz'=2,'row'=4,'col'=32] {'col'}, dimensions={1}, use_global_device_ids=true | all-gather | bytes 1584 | tf_op jit(solution)/shard_map/all_gather | solution.py:44
  89.1 0.1 iota_compare_fusion.3
  89.1 0.1 iota_compare_fusion.2
  89.2 0.0 all-gather.10.cloned.1.call-done
  89.2 11.1 %fusion.12 = bf16[64,4,128,128]{3,1,2,0:T(4,128)(2,1)} fusion(bf16[1,64,3,128,128]{4,3,2,0,1:T(8,128)(2,1)} %all-gather.10.cloned.1.call-done, s32[64,3]{1,0:T(8,128)S(1)} %bitcast.50, pred[64,3]{1,0:T(8,128)(4,1)S(1)} %iota_compare_fusion.2), kind=kOutput, calls=%fused_computation.11 | convolution fusion | flops 29361664 | bytes 14681024 | tf_op jit(solution)/shard_map/kcm,kcab->kamb/dot_general | solution.py:26
  100.3 102.7 %all-gather.8.cloned.1.call-done = bf16[64,6,128,128]{3,2,1,0:T(8,128)(2,1)} async-done(((bf16[2,6,128,128]{3,2,1,0:T(8,128)(2,1)}), bf16[64,6,128,128]{3,2,1,0:T(8,128)(2,1)}) %all-gather.8.cloned.1.call-update) | async-done | bytes 12582928 | tf_op jit(solution)/shard_map/all_gather | solution.py:44
  203.0 16.6 %convert_bitcast_fusion = bf16[8,128,64,128]{3,0,1,2:T(8,128)(2,1)} fusion(bf16[64,6,128,128]{3,2,1,0:T(8,128)(2,1)} %all-gather.8.cloned.1.call-done, s32[64,6]{1,0:T(8,128)S(1)} %bitcast.49, pred[64,6]{1,0:T(8,128)(4,1)S(1)} %iota_compare_fusion.3), kind=kOutput, calls=%fused_computation.5 | convolution fusion | flops 109058048 | bytes 29362048 | tf_op jit(solution)/shard_map/krl,krab->lakb/dot_general | solution.py:13
  219.7 0.0 copy-start.3
  219.7 18.9 %copy.16 = bf16[8,128,64,128]{3,2,1,0:T(8,128)(2,1)} copy(bf16[8,128,64,128]{3,0,1,2:T(8,128)(2,1)} %convert_bitcast_fusion) | data formatting | bytes 33554432 | tf_op jit(solution)/shard_map/convert_element_type | solution.py:13
  238.6 0.0 copy-done.3
  238.6 22.4 %fusion = f32[1024,512]{1,0:T(8,128)} fusion(bf16[128,8,64,128]{3,2,1,0:T(8,128)(2,1)} %bitcast.47, bf16[1024,8,4,128]{3,2,1,0:T(4,128)(2,1)S(1)} %bitcast.52), kind=kOutput, calls=%fused_computation | convolution fusion | flops 8589934592 | bytes 27262976 | tf_op jit(solution)/shard_map/dot_general | solution.py:46
  261.0 0.0 all-reduce.4.cloned.1.call-update
  261.0 30.8 %all-reduce.4.cloned.1.call-done = f32[1024,512]{1,0:T(8,128)} async-done(((f32[1024,512]{1,0:T(8,128)}), f32[1024,512]{1,0:T(8,128)}) %all-reduce.4.cloned.1.call-update) | async-done | bytes 2097168 | tf_op jit(solution)/shard_map/psum | solution.py:47
  291.8 0.0 copy-done.2
  291.8 3.4 %sub.3 = f32[1024,512]{1,0:T(8,128)} subtract(f32[1024,512]{1,0:T(8,128)S(1)} %copy-done.2, f32[1024,512]{1,0:T(8,128)} %all-reduce.4.cloned.1.call-done) | non-fusion elementwise | flops 524288 | bytes 6291456 | tf_op jit(solution)/shard_map/sub | solution.py:47
  295.2 0.0 copy-done.1
  (4 shorter events, 0.0 us)
Async XLA Ops:
  6.5 1.0 copy-start
  6.5 82.7 %all-gather.10.cloned.1.call-start = ((), (), s32[]{:S(2)}) async-start(), calls=%async_computation.2 | async-start | bytes 7864320 | tf_op jit(solution)/shard_map/all_gather | solution.py:42
  7.3 195.8 %all-gather.8.cloned.1.call-start = ((), (), s32[]{:S(2)}) async-start(), calls=%async_computation | async-start | bytes 12976128 | tf_op jit(solution)/shard_map/all_gather | solution.py:44
  9.4 282.4 %all-reduce.4.cloned.1.call-start = ((), (), s32[]{:S(2)}) async-start(), calls=%async_computation.1 | async-start | bytes 4194304 | tf_op jit(solution)/shard_map/psum | solution.py:47
  219.7 18.9 %copy-start.3 = (bf16[64,4,128,128]{3,1,2,0:T(4,128)(2,1)S(1)}, bf16[64,4,128,128]{3,1,2,0:T(4,128)(2,1)}, u32[]{:S(2)}) copy-start(bf16[64,4,128,128]{3,1,2,0:T(4,128)(2,1)} %fusion.12) | copy-start | bytes 25165828
  238.6 53.2 %copy-start.2 = (f32[1024,512]{1,0:T(8,128)S(1)}, f32[1024,512]{1,0:T(8,128)}, u32[]{:S(2)}) copy-start(f32[1024,512]{1,0:T(8,128)} %param.8) | copy-start | bytes 6291460
  238.6 56.6 %copy-start.1 = (bf16[1,2,6,128,128]{4,3,2,1,0:T(8,128)(2,1)S(1)}, bf16[1,2,6,128,128]{4,3,2,1,0:T(8,128)(2,1)}, u32[]{:S(2)}) copy-start(bf16[1,2,6,128,128]{4,3,2,1,0:T(8,128)(2,1)} %param.9) | copy-start | bytes 1179652
Sparse Core Ops, SparseCore 0:
  9.1 72.1 all-gather.9
  83.9 119.0 all-gather.7
  261.1 30.5 all-reduce.3
where the time goes:
time: 302 us
  waiting for transfers between devices  134 us (44%)
  blocking collectives  73.4 us (24%)
  matrix products  52 us (17%)
  local copies, waits for them, and re-layouts  24.1 us (8%)
  between operations  14.5 us (5%)
  other arithmetic  3.53 us (1%)
    all_gather x1, waiting for transfers between devices, on_device(): lax.all_gather((solved, row_ids[0], row_counts[0]), 'col', axis=0, tiled=...  103 us
    all_gather x1, blocking collectives, on_device(): lax.all_gather((solved, row_ids[0], row_counts[0]), 'col', axis=0, tiled=...  35 us
    psum x1, waiting for transfers between devices, on_device(): return ancestor - lax.psum(partial_sum, 'gz')  30.8 us
    unnamed x2, blocking collectives  27.7 us
    dot_general x1, matrix products, on_device(): jnp.dot(lower_dense, upper_dense, preferred_element_type=jnp.float32)  22.4 us
    convert_element_type x1, local copies, waits for them, and re-layouts, spread_rows(): jnp.einsum('krl,krab->lakb', select, tiles, preferred_element_type=jnp.fl...  18.9 us
    dot_general x1, matrix products, spread_rows(): jnp.einsum('krl,krab->lakb', select, tiles, preferred_element_type=jnp.fl...  16.6 us
    dot_general x1, matrix products, spread_cols(): jnp.einsum('kcm,kcab->kamb', select, tiles, preferred_element_type=jnp.fl...  11.1 us
  transfers between devices with their start and end apart: 3, of which 2 were waited for; matrix products, arithmetic and copies ran while one was open for 6% of the time, Pallas kernels for 0%

commit v1 on v0

--- a/solution.py
+++ b/solution.py
@@ -44,7 +44,7 @@
     piece = lax.all_gather((solved, row_ids[0], row_counts[0]), "col", axis=0, tiled=True)
     lower_dense = spread_rows(piece[0], piece[1], piece[2], row_blocks)
     partial_sum = jnp.dot(lower_dense, upper_dense, preferred_element_type=jnp.float32)
-    return ancestor - lax.psum(partial_sum, "gz")
+    return ancestor - jnp.sum(lax.all_gather(partial_sum, "gz"), axis=0)
 
 
 def solution(mesh):

time: 302 us -> 292 us (0.967)
  waiting for transfers between devices: 134 us -> 121 us
    psum x1 -> x0, waiting for transfers between devices: 30.8 us -> none  [on_device(): return ancestor - lax.psum(partial_sum, 'gz')]
    all_gather x0 -> x1, waiting for transfers between devices: none -> 17.7 us  [on_device(): return ancestor - jnp.sum(lax.all_gather(partial_sum, 'gz'), axis=0)]
where the time goes in v1:
time: 292 us; the launch traced here: 291 us
  waiting for transfers between devices  121 us (41%)
  blocking collectives  73.4 us (25%)
  matrix products  51.8 us (18%)
  local copies, waits for them, and re-layouts  24 us (8%)
  between operations  14.4 us (5%)
  other arithmetic  6.39 us (2%)
    all_gather x1, waiting for transfers between devices, on_device(): lax.all_gather((solved, row_ids[0], row_counts[0]), 'col', axis=0, tiled=...  103 us
    all_gather x1, blocking collectives, on_device(): lax.all_gather((solved, row_ids[0], row_counts[0]), 'col', axis=0, tiled=...  35 us
    unnamed x2, blocking collectives  27.7 us
    dot_general x1, matrix products, on_device(): jnp.dot(lower_dense, upper_dense, preferred_element_type=jnp.float32)  22.3 us
    convert_element_type x1, local copies, waits for them, and re-layouts, spread_rows(): jnp.einsum('krl,krab->lakb', select, tiles, preferred_element_type=jnp.fl...  18.9 us
    all_gather x1, waiting for transfers between devices, on_device(): return ancestor - jnp.sum(lax.all_gather(partial_sum, 'gz'), axis=0)  17.7 us
    dot_general x1, matrix products, spread_rows(): jnp.einsum('krl,krab->lakb', select, tiles, preferred_element_type=jnp.fl...  16.6 us
    dot_general x1, matrix products, spread_cols(): jnp.einsum('kcm,kcab->kamb', select, tiles, preferred_element_type=jnp.fl...  11.1 us
  transfers between devices with their start and end apart: 3, of which 2 were waited for; matrix products, arithmetic and copies ran while one was open for 6% of the time, Pallas kernels for 0%

profile of v1, /device:TPU:1, one launch (start us, length us, event | category | flops | bytes accessed | tf_op | source)
XLA Modules:
  0.0 291.3 jit_solution(788987961180053190)
XLA Ops:
  6.5 0.0 copy-start
  6.5 0.0 all-gather.12.cloned.1.call-start
  6.5 0.7 all-gather.12.cloned.1.call-update
  7.3 0.0 all-gather.10.cloned.1.call-start
  7.3 0.2 copy-done
  7.5 1.8 convolution_convert_fusion
  9.4 0.0 all-gather.10.cloned.1.call-update
  9.4 0.0 all-gather.14.cloned.1.call-start
  9.4 1.3 dynamic-slice
  10.8 1.3 dynamic-slice.1
  12.0 0.8 copy.17
  14.1 0.8 bitcast_dynamic-update-slice_fusion.1
  14.8 20.0 %all-reduce = s32[64]{0:T(128)S(1)} all-reduce(s32[64]{0:T(128)S(1)} %bitcast_dynamic-update-slice_fusion.1), channel_id=3, replica_groups=mesh['gz'=2,'row'=4,'col'=32] {'col'}, use_global_device_ids=true, to_apply=%add | all-reduce | flops 64 | bytes 512
  34.8 0.7 bitcast_dynamic-update-slice_fusion
  35.6 7.7 %all-reduce.1 = s32[64]{0:T(128)S(1)} all-reduce(s32[64]{0:T(128)S(1)} %bitcast_dynamic-update-slice_fusion), channel_id=5, replica_groups=mesh['gz'=2,'row'=4,'col'=32] {'row'}, use_global_device_ids=true, to_apply=%add.1 | all-reduce | flops 64 | bytes 512
  43.3 10.6 %all-gather.2 = s32[1,64,3]{2,0,1:T(1,128)S(1)} all-gather(s32[1,16,3]{2,0,1:T(1,128)S(1)} %copy.17), channel_id=4, replica_groups=mesh['gz'=2,'row'=4,'col'=32] {'row'}, dimensions={1}, use_global_device_ids=true | all-gather | bytes 960 | tf_op jit(solution)/shard_map/all_gather | solution.py:42
  53.9 35.0 %all-gather = s32[1,64,6]{2,0,1:T(1,128)S(1)} all-gather(s32[1,2,6]{2,0,1:T(1,128)} %bitcast.53), channel_id=2, replica_groups=mesh['gz'=2,'row'=4,'col'=32] {'col'}, dimensions={1}, use_global_device_ids=true | all-gather | bytes 1584 | tf_op jit(solution)/shard_map/all_gather | solution.py:44
  88.9 0.1 iota_compare_fusion.3
  89.0 0.1 iota_compare_fusion.2
  89.1 0.0 all-gather.12.cloned.1.call-done
  89.1 11.1 %fusion.12 = bf16[64,4,128,128]{3,1,2,0:T(4,128)(2,1)} fusion(bf16[1,64,3,128,128]{4,3,2,0,1:T(8,128)(2,1)} %all-gather.12.cloned.1.call-done, s32[64,3]{1,0:T(8,128)S(1)} %bitcast.52, pred[64,3]{1,0:T(8,128)(4,1)S(1)} %iota_compare_fusion.2), kind=kOutput, calls=%fused_computation.11 | convolution fusion | flops 29361664 | bytes 14681024 | tf_op jit(solution)/shard_map/kcm,kcab->kamb/dot_general | solution.py:26
  100.2 102.8 %all-gather.10.cloned.1.call-done = bf16[64,6,128,128]{3,2,1,0:T(8,128)(2,1)} async-done(((bf16[2,6,128,128]{3,2,1,0:T(8,128)(2,1)}), bf16[64,6,128,128]{3,2,1,0:T(8,128)(2,1)}) %all-gather.10.cloned.1.call-update) | async-done | bytes 12582928 | tf_op jit(solution)/shard_map/all_gather | solution.py:44
  203.0 16.6 %convert_bitcast_fusion = bf16[8,128,64,128]{3,0,1,2:T(8,128)(2,1)} fusion(bf16[64,6,128,128]{3,2,1,0:T(8,128)(2,1)} %all-gather.10.cloned.1.call-done, s32[64,6]{1,0:T(8,128)S(1)} %bitcast.51, pred[64,6]{1,0:T(8,128)(4,1)S(1)} %iota_compare_fusion.3), kind=kOutput, calls=%fused_computation.5 | convolution fusion | flops 109058048 | bytes 29362048 | tf_op jit(solution)/shard_map/krl,krab->lakb/dot_general | solution.py:13
  219.7 0.0 copy-start.2
  219.7 18.9 %copy.16 = bf16[8,128,64,128]{3,2,1,0:T(8,128)(2,1)} copy(bf16[8,128,64,128]{3,0,1,2:T(8,128)(2,1)} %convert_bitcast_fusion) | data formatting | bytes 33554432 | tf_op jit(solution)/shard_map/convert_element_type | solution.py:13
  238.6 0.0 copy-done.2
  238.6 22.3 %fusion = f32[1024,512]{1,0:T(8,128)} fusion(bf16[128,8,64,128]{3,2,1,0:T(8,128)(2,1)} %bitcast.48, bf16[1024,8,4,128]{3,2,1,0:T(4,128)(2,1)S(1)} %bitcast.54), kind=kOutput, calls=%fused_computation | convolution fusion | flops 8589934592 | bytes 27262976 | tf_op jit(solution)/shard_map/dot_general | solution.py:46
  260.8 0.0 all-gather.14.cloned.1.call-update
  260.9 17.7 %all-gather.14.cloned.1.call-done = f32[2048,512]{1,0:T(8,128)} async-done(((f32[1024,512]{1,0:T(8,128)}), f32[2048,512]{1,0:T(8,128)}) %all-gather.14.cloned.1.call-update) | async-done | bytes 4194320 | tf_op jit(solution)/shard_map/all_gather | solution.py:47
  278.5 2.9 reduce_sum.9
  281.4 3.4 %sub.3 = f32[1024,512]{1,0:T(8,128)} subtract(f32[1024,512]{1,0:T(8,128)} %param.8, f32[1024,512]{1,0:T(8,128)S(1)} %reduce_sum.9) | non-fusion elementwise | flops 524288 | bytes 6291456 | tf_op jit(solution)/shard_map/sub | solution.py:47
  284.8 0.0 copy-done.1
  (3 shorter events, 0.0 us)
Async XLA Ops:
  6.5 1.0 copy-start
  6.5 82.6 %all-gather.12.cloned.1.call-start = ((), (), s32[]{:S(2)}) async-start(), calls=%async_computation.1 | async-start | bytes 7864320 | tf_op jit(solution)/shard_map/all_gather | solution.py:42
  7.3 195.8 %all-gather.10.cloned.1.call-start = ((), (), s32[]{:S(2)}) async-start(), calls=%async_computation | async-start | bytes 12976128 | tf_op jit(solution)/shard_map/all_gather | solution.py:44
  9.4 269.1 %all-gather.14.cloned.1.call-start = ((), (), s32[]{:S(2)}) async-start(), calls=%async_computation.2 | async-start | bytes 6291456 | tf_op jit(solution)/shard_map/all_gather | solution.py:47
  219.7 18.9 %copy-start.2 = (bf16[64,4,128,128]{3,1,2,0:T(4,128)(2,1)S(1)}, bf16[64,4,128,128]{3,1,2,0:T(4,128)(2,1)}, u32[]{:S(2)}) copy-start(bf16[64,4,128,128]{3,1,2,0:T(4,128)(2,1)} %fusion.12) | copy-start | bytes 25165828
  238.6 46.2 %copy-start.1 = (bf16[1,2,6,128,128]{4,3,2,1,0:T(8,128)(2,1)S(1)}, bf16[1,2,6,128,128]{4,3,2,1,0:T(8,128)(2,1)}, u32[]{:S(2)}) copy-start(bf16[1,2,6,128,128]{4,3,2,1,0:T(8,128)(2,1)} %param.9) | copy-start | bytes 1179652
Sparse Core Ops, SparseCore 0:
  9.1 72.1 all-gather.11
  83.9 119.0 all-gather.9
  261.0 17.5 all-gather.13
